TPU v7x, 32 devices: a whole 2x2x4 slice. The times are simulated.
32 devices in a mesh: ctx: 16 (over z, x, core), ch: 2 (over y).
Axes of the slice: x: 2, y: 2, z: 4, core: 2. Of those that a mesh axis runs over, the one named last changes fastest.
Arguments:
- q_proj: bfloat16 [512, 16384], P('ch', 'ctx'), may hold values from -6 to 6
- k_proj: bfloat16 [512, 16384], P('ch', 'ctx'), may hold values from -6 to 6
- v_proj: bfloat16 [512, 16384], P('ch', 'ctx'), may hold values from -6 to 6
- short_taps: bfloat16 [3, 512, 3], P(None, 'ch'), may hold values from -3.5 to 3.5
- long_filter: float32 [512, 16384], P('ch', 'ctx'), may hold values from -4 to 4
- skip_gain: float32 [512], P('ch'), may hold values from 0.5 to 1.5
- out_weight: bfloat16 [512, 4096], P(None, 'ch'), may hold values from -0.25 to 0.25
Outputs:
- block_out: bfloat16 [16384, 4096], P('ctx', 'ch')
All inputs are finite; a program needn't handle non-finite values.
Results may differ from a plain program's by a relative error of at most 0.012.
Values may be sent and summed in bfloat16 or wider, within the bound.
No kernel may reach another device: no remote copies, remote signals or barrier semaphores. Data moves between devices by JAX's collectives and lax.ppermute only.
A program may use at most 128 MiB of HBM per device.

v0:
```python
import functools
import math

import jax
import jax.numpy as jnp
import numpy as np
from jax import lax
from jax.experimental import pallas as pl
from jax.experimental.pallas import tpu as pltpu
from jax.sharding import PartitionSpec as P

LANES = 128
GROUP = 8
STEPS = 2
f32, bf16 = jnp.float32, jnp.bfloat16


def split_table(table):
    high = table.astype(jnp.bfloat16)
    low = (table - high.astype(np.float64)).astype(jnp.bfloat16)
    return np.stack([high, low])


def thrice(table, axis):
    high, low = split_table(table)
    return np.concatenate([high, high, low], axis)


def transform_tables(n1):
    shifted = np.arange(n1)[:, None] + 0.25
    angle = -2 * np.pi * shifted * np.arange(n1)[None, :] / n1
    first = split_table(np.concatenate([np.cos(angle), np.sin(angle)], 0))
    twist = -2 * np.pi * shifted * np.arange(LANES)[None, :] / (n1 * LANES)
    lane = np.arange(LANES)
    inner = -2 * np.pi * (lane[:, None] * lane[None, :] % LANES) / LANES
    c, s = np.cos(inner), np.sin(inner)
    return dict(
        first=np.concatenate([first[0], first[1]], 1),
        twist=np.stack([np.cos(twist), np.sin(twist)]).astype(np.float32),
        forward=thrice(np.block([[c, s], [-s, c]]), 0),
        inverse=thrice(np.block([[c, -s], [s, c]]) / LANES, 0),
        last=thrice(np.concatenate([np.cos(angle.T), np.sin(angle.T)], 1) / n1, 1),
    )


def split(x):
    high = x.astype(bf16)
    return high, (x - high.astype(f32)).astype(bf16)


def dot(a, b):
    return lax.dot_general(a, b, (((1,), (0,)), ((), ())), preferred_element_type=f32)


def dot_table(x, table):
    high, low = split(x)
    return dot(jnp.concatenate([high, low, high], 1), table[...])


def rows_by_channel(source, scratch, channels, count, rows, n1, order=None, base=0):
    for s in range(count):
        block = source[s].astype(f32)
        first = (base + s) * rows if order is None else pl.multiple_of(order[base + s] * rows, rows)
        for r in range(rows):
            scratch[pl.ds(first + r, channels, stride=n1), :] = block[:, r * LANES : (r + 1) * LANES]


def groups_of(channels, size):
    return [list(range(i, min(i + size, channels))) for i in range(0, channels, size)]


def forward_transform(planes, first, twist, forward, group, n1):
    tc, ts = twist[0], twist[1]
    stacked = [[] for _ in planes]
    for c in group:
        x = jnp.concatenate([plane[c * n1 : (c + 1) * n1, :].astype(bf16) for plane in planes], 1)
        a = dot(first[...], jnp.concatenate([x, x], 0))
        for p in range(len(planes)):
            re, im = a[:n1, p * LANES : (p + 1) * LANES], a[n1:, p * LANES : (p + 1) * LANES]
            stacked[p].append(jnp.concatenate([re * tc - im * ts, re * ts + im * tc], 1))
    return dot_table(jnp.concatenate(sum(stacked, []), 0), forward)


def start_copies(sources, targets, sems, base=0):
    copies = [pltpu.make_async_copy(x, y, sems.at[base + i]) for i, (x, y) in enumerate(zip(sources, targets))]
    for copy in copies:
        copy.start()
    return copies


def conv_kernel(order, *refs, count, channels, sources, rows):
    arrived, u, tables, out = refs[:count], refs[count], refs[count + 1 : count + 6], refs[count + 6]
    moved, held, first, twist, forward, inverse, last, h_plane, u_plane, sems = refs[count + 7 :]
    n1 = sources * rows
    each = sources // count
    parts = [pl.ds(i * each, each) for i in range(count)]
    inputs = start_copies(list(arrived) + [u.at[p] for p in parts], [moved.at[p] for p in parts] + [held.at[p] for p in parts], sems)
    filled = start_copies(tables, (first, twist, forward, inverse, last), sems, 2 * count)
    for i in range(count):
        inputs[i].wait()
        rows_by_channel(moved.at[parts[i]], h_plane, channels, each, rows, n1, order, i * each)
    for i in range(count):
        inputs[count + i].wait()
        rows_by_channel(held.at[parts[i]], u_plane, channels, each, rows, n1, base=i * each)
    for copy in filled:
        copy.wait()
    tc, ts = twist[0], twist[1]
    for group in groups_of(channels, GROUP):
        both = forward_transform((u_plane, h_plane), first, twist, forward, group, n1)
        spec, other = both[: len(group) * n1], both[len(group) * n1 :]
        xr, xi, hr, hi = spec[:, :LANES], spec[:, LANES:], other[:, :LANES], other[:, LANES:]
        back = dot_table(jnp.concatenate([xr * hr - xi * hi, xr * hi + xi * hr], 1), inverse)
        for pair in groups_of(len(group), 2):
            columns = []
            for p in pair:
                br, bi = back[p * n1 : (p + 1) * n1, :LANES], back[p * n1 : (p + 1) * n1, LANES:]
                high, low = split(jnp.concatenate([br * tc + bi * ts, bi * tc - br * ts], 0))
                columns.append(jnp.concatenate([high, low, high], 0))
            y = dot(last[...], jnp.concatenate(columns, 1))
            for i, p in enumerate(pair):
                u_plane[group[p] * n1 : (group[p] + 1) * n1, :] = y[:, i * LANES : (i + 1) * LANES]
    for s in range(sources):
        for r in range(rows):
            piece = u_plane[pl.ds(s * rows + r, channels, stride=n1), :]
            out[s, :, r * LANES : (r + 1) * LANES] = piece.astype(out.dtype)


def edge_kernel(q, k, v, out, *, width):
    rows = [x[...].astype(f32).T[LANES - width :, :] for x in (q, k, v)]
    rows.append(jnp.zeros((out.shape[0] - 3 * width, out.shape[1]), f32))
    out[...] = jnp.concatenate(rows, 0).astype(out.dtype)


def edges(q, k, v, width):
    channels, tokens = q.shape
    block = pl.BlockSpec((channels, LANES), lambda i: (0, tokens // LANES - 1))
    return pl.pallas_call(
        functools.partial(edge_kernel, width=width),
        grid=(1,),
        in_specs=[block] * 3,
        out_specs=pl.BlockSpec((16, channels), lambda i: (0, 0)),
        out_shape=jax.ShapeDtypeStruct((16, channels), bf16),
        compiler_params=room(8),
        name="edges",
    )(*in_hbm(q, k, v))


def filtered(x, taps, rim, width):
    lane = lax.broadcasted_iota(jnp.int32, x.shape, 1)
    total = taps[:, :1] * x
    for back in range(1, width + 1):
        moved = pltpu.roll(x, back, 1)
        for i in range(back):
            moved = jnp.where(lane == i, rim[:, width - back + i : width - back + i + 1], moved)
        total = total + taps[:, back : back + 1] * moved
    return total


def columns_of(*arrays):
    rows = [x.astype(f32) for x in arrays]
    count = sum(x.shape[0] for x in rows)
    rows.append(jnp.zeros((LANES - count, rows[0].shape[1]), f32))
    return jnp.concatenate(rows, 0).T


def pair_kernel(k, v, taps, rim, out, *, width):
    span = width + 1
    columns = columns_of(rim[...], taps[1], taps[2])
    base = rim.shape[0]
    ks = filtered(k[...].astype(f32), columns[:, base : base + span], columns[:, width : 2 * width], width)
    vs = filtered(v[...].astype(f32), columns[:, base + span : base + 2 * span], columns[:, 2 * width : 3 * width], width)
    out[...] = (ks * vs).astype(out.dtype)


def query_kernel(q, taps, rim, out, *, width):
    columns = columns_of(rim[...], taps[0])
    base = rim.shape[0]
    out[...] = filtered(q[...].astype(f32), columns[:, base : base + width + 1], columns[:, :width], width)


def featurize(kernel, arrays, tap_rows, rim, dtype):
    channels, tokens = arrays[0].shape
    size = channels // STEPS if channels % (STEPS * LANES) == 0 else channels
    rows = pl.BlockSpec((size, tokens), lambda i: (i, 0))
    return pl.pallas_call(
        functools.partial(kernel, width=tap_rows.shape[1] - 1),
        grid=(channels // size,),
        in_specs=[rows] * len(arrays)
        + [
            pl.BlockSpec(tap_rows.shape[:2] + (size,), lambda i: (0, 0, i)),
            pl.BlockSpec((rim.shape[0], size), lambda i: (0, i)),
        ],
        out_specs=rows,
        out_shape=jax.ShapeDtypeStruct((channels, tokens), dtype),
        compiler_params=room(12),
    )(*in_hbm(*arrays), tap_rows, rim)


def pack_kernel(inner_index, *refs, count, inner, own):
    pieces, outs = refs[:count], refs[count:]
    for step in range(inner):
        begin = pl.multiple_of(((inner_index[0] + step) % inner) * own, own)
        for i in range(count):
            outs[step][i] = pieces[i][pl.ds(begin, own), :]


def in_hbm(*values):
    return [pltpu.with_memory_space_constraint(value, pltpu.HBM) for value in values]


def room(mebibytes):
    return pltpu.CompilerParams(vmem_limit_bytes=mebibytes << 20)


def smem():
    return pl.BlockSpec(memory_space=pltpu.SMEM)


def vmem():
    return pl.BlockSpec(memory_space=pltpu.VMEM)


def moved_filter(long_filter, sources, own):
    tokens = long_filter.shape[1]
    inner = max(d for d in range(1, int(math.isqrt(sources)) + 1) if sources % d == 0)
    outer = sources // inner
    group = own * inner
    me = lax.axis_index("ctx")
    me_outer, me_inner = me // inner, me % inner

    def outer_pairs(step):
        return [(i, (i // inner + step) % outer * inner + i % inner) for i in range(sources)]

    def inner_pairs(step):
        return [(i, i // inner * inner + (i % inner + step) % inner) for i in range(sources)]

    pieces = []
    for step in range(outer):
        piece = lax.dynamic_slice_in_dim(long_filter, (me_outer + step) % outer * group, group, 0).astype(bf16)
        pieces.append(piece if step == 0 else lax.ppermute(piece, "ctx", outer_pairs(step)))
    if own % 16 == 0:
        packed = pl.pallas_call(
            functools.partial(pack_kernel, count=outer, inner=inner, own=own),
            in_specs=[smem()] + [vmem()] * outer,
            out_specs=[vmem()] * inner,
            out_shape=[jax.ShapeDtypeStruct((outer, own, tokens), bf16)] * inner,
            compiler_params=room(8),
            name="pack",
        )(me_inner[None].astype(jnp.int32), *pieces)
    else:
        stacked = jnp.stack(pieces)
        packed = [
            lax.dynamic_slice_in_dim(stacked, (me_inner + step) % inner * own, own, 1) for step in range(inner)
        ]
    arrived = [packed[0]] + [lax.ppermute(packed[step], "ctx", inner_pairs(step)) for step in range(1, inner)]
    order = ((me_outer - jnp.arange(outer))[None, :] % outer) * inner + ((me_inner - jnp.arange(inner)) % inner)[:, None]
    return arrived, order.reshape(-1).astype(jnp.int32)


def block(q_proj, k_proj, v_proj, short_taps, long_filter, skip_gain, out_weight):
    channels, tokens = q_proj.shape
    width = short_taps.shape[2] - 1
    tap_rows = jnp.swapaxes(short_taps, 1, 2)
    sources = lax.axis_size("ctx")
    own = channels // sources
    halves = lax.axis_size("ch")
    n1 = sources * tokens // LANES
    tables = {name: jnp.asarray(t) for name, t in transform_tables(n1).items()}

    rim = lax.ppermute(edges(q_proj, k_proj, v_proj, width), "ctx", [(i, i + 1) for i in range(sources - 1)])
    arrived, order = moved_filter(long_filter, sources, own)
    product_kv = featurize(pair_kernel, (k_proj, v_proj), tap_rows, rim, bf16)
    signal_moved = lax.all_to_all(product_kv.reshape(sources, own, tokens), "ctx", 0, 0)
    q_short = featurize(query_kernel, (q_proj,), tap_rows, rim, f32)

    plane = pltpu.VMEM((own * n1, LANES), f32)
    used = [tables[name] for name in ("first", "twist", "forward", "inverse", "last")]
    count = len(arrived)
    result = pl.pallas_call(
        functools.partial(conv_kernel, count=count, channels=own, sources=sources, rows=tokens // LANES),
        in_specs=[smem()] + [pl.BlockSpec(memory_space=pl.ANY)] * (count + 1 + len(used)),
        out_specs=vmem(),
        out_shape=jax.ShapeDtypeStruct(signal_moved.shape, bf16),
        scratch_shapes=[pltpu.VMEM(signal_moved.shape, bf16)] * 2
        + [pltpu.VMEM(t.shape, t.dtype) for t in used]
        + [plane, plane, pltpu.SemaphoreType.DMA((2 * count + len(used),))],
        compiler_params=room(40),
        name="convolve",
    )(order, *arrived, signal_moved, *in_hbm(*used))
    long_out = lax.all_to_all(result, "ctx", 0, 0).reshape(channels, tokens).astype(f32)
    gated = (q_short * (long_out + skip_gain[:, None] * product_kv.astype(f32))).astype(bf16)

    mine = lax.axis_index("ch")
    summed = None
    for step in range(halves):
        piece = gated if step == 0 else lax.ppermute(gated, "ch", [(i, (i + step) % halves) for i in range(halves)])
        owner = (mine - step) % halves
        weights = lax.dynamic_slice_in_dim(out_weight, owner * channels, channels, axis=0)
        part = jnp.einsum("cb,cd->bd", piece, weights, preferred_element_type=f32)
        summed = part if summed is None else summed + part
    return summed.astype(bf16)


def solution(mesh):
    in_specs = (P("ch", "ctx"), P("ch", "ctx"), P("ch", "ctx"), P(None, "ch", None), P("ch", "ctx"), P("ch"), P(None, "ch"))
    return jax.shard_map(block, mesh=mesh, in_specs=in_specs, out_specs=P("ctx", "ch"), check_vma=False)
```

profile of v0, /device:TPU:0, one launch (start us, length us, event | category | flops | bytes accessed | tf_op | source)
XLA Modules:
  0.0 104.4 jit_solution(16133410066109899265)
XLA Ops:
  0.0 0.0 copy-start
  0.0 0.0 copy-start.2
  0.0 1.2 %edges.1 = bf16[16,256]{1,0:T(8,128)(2,1)S(1)} custom-call(bf16[256,1024]{1,0:T(8,128)(2,1)} %q.3, bf16[256,1024]{1,0:T(8,128)(2,1)} %k.3, bf16[256,1024]{1,0:T(8,128)(2,1)} %v.3), custom_call_target="tpu_custom_call" | custom-call | tf_op jit(solution)/shard_map/edges/pallas_call | solution.py:137
  1.2 2.4 %collective-permute-start = (bf16[16,256]{1,0:T(8,128)(2,1)S(1)}, bf16[16,256]{1,0:T(8,128)(2,1)S(1)}, u32[]{:S(2)}, u32[]{:S(2)}) collective-permute-start(bf16[16,256]{1,0:T(8,128)(2,1)S(1)} %edges.1), channel_id=1, source_target_pairs={{0,2},{2,4},{4,6},{6,8},{8,10},{10,12},{12,14},{14,16},{16,18},{18... | collective-permute-start | bytes 24584 | tf_op jit(solution)/shard_map/ppermute | solution.py:270
  3.6 0.8 collective-permute-done.rim
  4.4 0.0 copy-start.1
  4.4 0.7 copy-done.1
  5.1 3.2 %shard_map.119 = bf16[256,1024]{1,0:T(8,128)(2,1)} custom-call(bf16[256,1024]{1,0:T(8,128)(2,1)} %k.3, bf16[256,1024]{1,0:T(8,128)(2,1)} %v.3, bf16[3,3,256]{2,1,0:T(4,128)(2,1)S(1)} %bitcast.8, bf16[16,256]{1,0:T(8,128)(2,1)S(1)} %collective-permute-done.rim), custom_call_target="tpu_custom_call" | custom-call | tf_op jit(solution)/shard_map/pallas_call | solution.py:185
  8.3 9.1 %all-to-all-start = ((bf16[16,16,1024]{2,1,0:T(8,128)(2,1)}), bf16[16,16,1024]{2,1,0:T(8,128)(2,1)S(1)}, u32[]{:S(2)}, u32[]{:S(2)}) async-start(bf16[16,16,1024]{2,1,0:T(8,128)(2,1)} %bitcast.2), calls=%async_computation | async-start | bytes 1048576 | tf_op jit(solution)/shard_map/all_to_all | solution.py:273
  17.5 1.3 %dynamic-slice_convert_fusion = (bf16[64,1024]{1,0:T(8,128)(2,1)S(1)}, bf16[64,1024]{1,0:T(8,128)(2,1)S(1)}, bf16[64,1024]{1,0:T(8,128)(2,1)S(1)}, bf16[64,1024]{1,0:T(8,128)(2,1)S(1)}) fusion(f32[256,1024]{1,0:T(8,128)} %param.16, s32[]{:T(128)S(6)} %select_n.85, s32[]{:T(128)S(6)} %select_n.81, s32[]{:T(128)S(6)} %select_n.79, s32[]{:T(128)S(6)} %select_n.83), kind=kLoop, calls=%fused_computation.7 | loop fusion | bytes 1048592 | tf_op jit(solution)/shard_map/convert_element_type | solution.py:239
  18.8 3.7 %collective-permute-start.3 = (bf16[64,1024]{1,0:T(8,128)(2,1)S(1)}, bf16[64,1024]{1,0:T(8,128)(2,1)S(1)}, u32[]{:S(2)}, u32[]{:S(2)}) collective-permute-start(bf16[64,1024]{1,0:T(8,128)(2,1)S(1)} %get-tuple-element.13), channel_id=1, source_target_pairs={{0,24},{2,26},{4,28},{6,30},{8,0},{10,2},{12,4},{14,6},{16,8},{18,... | collective-permute-start | bytes 393224 | tf_op jit(solution)/shard_map/ppermute | solution.py:240
  22.5 0.0 collective-permute-start.1
  22.5 1.1 %collective-permute-start.2 = (bf16[64,1024]{1,0:T(8,128)(2,1)S(1)}, bf16[64,1024]{1,0:T(8,128)(2,1)S(1)}, u32[]{:S(2)}, u32[]{:S(2)}) collective-permute-start(bf16[64,1024]{1,0:T(8,128)(2,1)S(1)} %get-tuple-element.16), channel_id=1, source_target_pairs={{0,16},{2,18},{4,20},{6,22},{8,24},{10,26},{12,28},{14,30},{16,0},... | collective-permute-start | bytes 393224 | tf_op jit(solution)/shard_map/ppermute | solution.py:240
  23.6 8.1 %collective-permute-done.3.refs_3_ = bf16[64,1024]{1,0:T(8,128)(2,1)S(1)} collective-permute-done((bf16[64,1024]{1,0:T(8,128)(2,1)S(1)}, bf16[64,1024]{1,0:T(8,128)(2,1)S(1)}, u32[]{:S(2)}, u32[]{:S(2)}) %collective-permute-start.3) | collective-permute-done | bytes 131104 | tf_op jit(solution)/shard_map/ppermute | solution.py:240
  31.7 5.4 %collective-permute-done.1.refs_1_ = bf16[64,1024]{1,0:T(8,128)(2,1)S(1)} collective-permute-done((bf16[64,1024]{1,0:T(8,128)(2,1)S(1)}, bf16[64,1024]{1,0:T(8,128)(2,1)S(1)}, u32[]{:S(2)}, u32[]{:S(2)}) %collective-permute-start.1) | collective-permute-done | bytes 131104 | tf_op jit(solution)/shard_map/ppermute | solution.py:240
  37.1 6.8 %collective-permute-done.2.refs_2_ = bf16[64,1024]{1,0:T(8,128)(2,1)S(1)} collective-permute-done((bf16[64,1024]{1,0:T(8,128)(2,1)S(1)}, bf16[64,1024]{1,0:T(8,128)(2,1)S(1)}, u32[]{:S(2)}, u32[]{:S(2)}) %collective-permute-start.2) | collective-permute-done | bytes 131104 | tf_op jit(solution)/shard_map/ppermute | solution.py:240
  43.9 0.7 pack.1
  44.6 0.0 collective-permute-start.4
  44.6 1.5 %collective-permute-start.5 = (bf16[4,16,1024]{2,1,0:T(8,128)(2,1)S(1)}, bf16[4,16,1024]{2,1,0:T(8,128)(2,1)S(1)}, u32[]{:S(2)}, u32[]{:S(2)}) collective-permute-start(bf16[4,16,1024]{2,1,0:T(8,128)(2,1)S(1)} %get-tuple-element.11), channel_id=1, source_target_pairs={{0,4},{2,6},{4,0},{6,2},{8,12},{10,14},{12,8},{14,10},{16,20},{18,... | collective-permute-start | bytes 393224 | tf_op jit(solution)/shard_map/ppermute | solution.py:255
  46.1 1.5 %collective-permute-start.6 = (bf16[4,16,1024]{2,1,0:T(8,128)(2,1)S(1)}, bf16[4,16,1024]{2,1,0:T(8,128)(2,1)S(1)}, u32[]{:S(2)}, u32[]{:S(2)}) collective-permute-start(bf16[4,16,1024]{2,1,0:T(8,128)(2,1)S(1)} %get-tuple-element.12), channel_id=1, source_target_pairs={{0,6},{2,0},{4,2},{6,4},{8,14},{10,8},{12,10},{14,12},{16,22},{18,... | collective-permute-start | bytes 393224 | tf_op jit(solution)/shard_map/ppermute | solution.py:255
  47.5 0.1 broadcast_add_fusion
  47.6 0.1 add.101.order
  47.7 2.6 %collective-permute-done.4.refs_1_ = bf16[4,16,1024]{2,1,0:T(8,128)(2,1)S(1)} collective-permute-done((bf16[4,16,1024]{2,1,0:T(8,128)(2,1)}, bf16[4,16,1024]{2,1,0:T(8,128)(2,1)S(1)}, u32[]{:S(2)}, u32[]{:S(2)}) %collective-permute-start.4) | collective-permute-done | bytes 131104 | tf_op jit(solution)/shard_map/ppermute | solution.py:255
  50.2 0.7 collective-permute-done.5.refs_2_
  51.0 1.4 %collective-permute-done.6.refs_3_ = bf16[4,16,1024]{2,1,0:T(8,128)(2,1)S(1)} collective-permute-done((bf16[4,16,1024]{2,1,0:T(8,128)(2,1)S(1)}, bf16[4,16,1024]{2,1,0:T(8,128)(2,1)S(1)}, u32[]{:S(2)}, u32[]{:S(2)}) %collective-permute-start.6) | collective-permute-done | bytes 131104 | tf_op jit(solution)/shard_map/ppermute | solution.py:255
  52.4 0.0 all-to-all-done.refs_4_
  52.4 11.2 %convolve.1 = bf16[16,16,1024]{2,1,0:T(8,128)(2,1)} custom-call(s32[16]{0:T(128)S(1)} %add.101.order, bf16[4,16,1024]{2,1,0:T(8,128)(2,1)S(1)} %get-tuple-element.9.refs_0_, bf16[4,16,1024]{2,1,0:T(8,128)(2,1)S(1)} %collective-permute-done.4.refs_1_, bf16[4,16,1024]{2,1,0:T(8,128)(2,1)S(1)} %collective-permute-done.5.refs_2_, ...), custom_call_target="tpu_custom_call" | custom-call | tf_op jit(solution)/shard_map/convolve/pallas_call | solution.py:279
  63.6 4.4 %all-to-all-start.1 = ((bf16[16,16,1024]{2,1,0:T(8,128)(2,1)}), bf16[16,16,1024]{2,1,0:T(8,128)(2,1)}, u32[]{:S(2)}, u32[]{:S(2)}) async-start(bf16[16,16,1024]{2,1,0:T(8,128)(2,1)} %convolve.1), calls=%async_computation.1 | async-start | bytes 1048576 | tf_op jit(solution)/shard_map/all_to_all | solution.py:290
  68.1 0.0 copy-done.2
  68.1 1.8 %shard_map.118 = f32[256,1024]{1,0:T(8,128)S(1)} custom-call(bf16[256,1024]{1,0:T(8,128)(2,1)} %q.3, bf16[3,3,256]{2,1,0:T(4,128)(2,1)S(1)} %bitcast.9, bf16[16,256]{1,0:T(8,128)(2,1)S(1)} %collective-permute-done.rim), custom_call_target="tpu_custom_call" | custom-call | tf_op jit(solution)/shard_map/pallas_call | solution.py:185
  70.0 12.3 %all-to-all-done.1 = bf16[16,16,1024]{2,1,0:T(8,128)(2,1)} async-done(((bf16[16,16,1024]{2,1,0:T(8,128)(2,1)}), bf16[16,16,1024]{2,1,0:T(8,128)(2,1)}, u32[]{:S(2)}, u32[]{:S(2)}) %all-to-all-start.1) | async-done | bytes 524320 | tf_op jit(solution)/shard_map/all_to_all | solution.py:290
  82.2 2.3 %fusion.1 = bf16[256,1024]{1,0:T(8,128)(2,1)} fusion(f32[256,1024]{1,0:T(8,128)S(1)} %shard_map.118, bf16[256,1024]{1,0:T(8,128)(2,1)} %shard_map.119, bf16[16,16,1024]{2,1,0:T(8,128)(2,1)} %all-to-all-done.1, f32[256]{0:T(256)} %param.17), kind=kLoop, calls=%fused_computation.3 | loop fusion | flops 1572864 | bytes 2622464 | tf_op jit(solution)/shard_map/convert_element_type | solution.py:291
  84.5 1.5 %collective-permute-start.7 = (bf16[256,1024]{1,0:T(8,128)(2,1)}, bf16[256,1024]{1,0:T(8,128)(2,1)S(1)}, u32[]{:S(2)}, u32[]{:S(2)}) collective-permute-start(bf16[256,1024]{1,0:T(8,128)(2,1)} %fusion.1), channel_id=1, source_target_pairs={{0,1},{1,0},{2,3},{3,2},{4,5},{5,4},{6,7},{7,6},{8,9},{9,8},{10,11... | collective-permute-start | bytes 1572872 | tf_op jit(solution)/shard_map/ppermute | solution.py:296
  86.0 12.7 %collective-permute-done.7 = bf16[256,1024]{1,0:T(8,128)(2,1)S(1)} collective-permute-done((bf16[256,1024]{1,0:T(8,128)(2,1)}, bf16[256,1024]{1,0:T(8,128)(2,1)S(1)}, u32[]{:S(2)}, u32[]{:S(2)}) %collective-permute-start.7) | collective-permute-done | bytes 524320 | tf_op jit(solution)/shard_map/ppermute | solution.py:296
  98.7 0.0 copy-done
  98.7 1.3 %fusion.2 = f32[1024,2048]{1,0:T(8,128)S(1)} fusion(bf16[256,1024]{1,0:T(8,128)(2,1)S(1)} %collective-permute-done.7, bf16[512,2048]{1,0:T(8,128)(2,1)S(1)} %copy-done, s32[]{:T(128)S(6)} %select_n.89), kind=kOutput, calls=%fused_computation.4 | convolution fusion | flops 1073741824 | bytes 9961476 | tf_op jit(solution)/shard_map/cb,cd->bd/dot_general | solution.py:299
  100.0 4.4 %add_convert_fusion = bf16[1024,2048]{1,0:T(8,128)(2,1)} fusion(f32[1024,2048]{1,0:T(8,128)S(1)} %fusion.2, bf16[256,1024]{1,0:T(8,128)(2,1)} %fusion.1, bf16[512,2048]{1,0:T(8,128)(2,1)S(1)} %copy-done, s32[]{:T(128)S(6)} %select_n.87), kind=kOutput, calls=%fused_computation | convolution fusion | flops 1077936128 | bytes 14155780 | tf_op jit(solution)/shard_map/cb,cd->bd/dot_general | solution.py:299
  (1 shorter events, 0.0 us)
Async XLA Ops:
  0.0 98.7 %copy-start = (bf16[512,2048]{1,0:T(8,128)(2,1)S(1)}, bf16[512,2048]{1,0:T(8,128)(2,1)}, u32[]{:S(2)}) copy-start(bf16[512,2048]{1,0:T(8,128)(2,1)} %param.18) | copy-start | bytes 6291460
  0.0 68.1 %copy-start.2 = (bf16[3,256,3]{1,2,0:T(4,128)(2,1)S(1)}, bf16[3,256,3]{1,2,0:T(4,128)(2,1)}, u32[]{:S(2)}) copy-start(bf16[3,256,3]{1,2,0:T(4,128)(2,1)} %param.15) | copy-start | bytes 13828
  1.2 3.2 %collective-permute-start = (bf16[16,256]{1,0:T(8,128)(2,1)S(1)}, bf16[16,256]{1,0:T(8,128)(2,1)S(1)}, u32[]{:S(2)}, u32[]{:S(2)}) collective-permute-start(bf16[16,256]{1,0:T(8,128)(2,1)S(1)} %edges.1), channel_id=1, source_target_pairs={{0,2},{2,4},{4,6},{6,8},{8,10},{10,12},{12,14},{14,16},{16,18},{18... | collective-permute-start | bytes 24584 | tf_op jit(solution)/shard_map/ppermute | solution.py:270
  4.4 0.7 copy-start.1
  8.3 44.1 %all-to-all-start = ((bf16[16,16,1024]{2,1,0:T(8,128)(2,1)}), bf16[16,16,1024]{2,1,0:T(8,128)(2,1)S(1)}, u32[]{:S(2)}, u32[]{:S(2)}) async-start(bf16[16,16,1024]{2,1,0:T(8,128)(2,1)} %bitcast.2), calls=%async_computation | async-start | bytes 1048576 | tf_op jit(solution)/shard_map/all_to_all | solution.py:273
  18.8 12.9 %collective-permute-start.3 = (bf16[64,1024]{1,0:T(8,128)(2,1)S(1)}, bf16[64,1024]{1,0:T(8,128)(2,1)S(1)}, u32[]{:S(2)}, u32[]{:S(2)}) collective-permute-start(bf16[64,1024]{1,0:T(8,128)(2,1)S(1)} %get-tuple-element.13), channel_id=1, source_target_pairs={{0,24},{2,26},{4,28},{6,30},{8,0},{10,2},{12,4},{14,6},{16,8},{18,... | collective-permute-start | bytes 393224 | tf_op jit(solution)/shard_map/ppermute | solution.py:240
  22.5 14.6 %collective-permute-start.1 = (bf16[64,1024]{1,0:T(8,128)(2,1)S(1)}, bf16[64,1024]{1,0:T(8,128)(2,1)S(1)}, u32[]{:S(2)}, u32[]{:S(2)}) collective-permute-start(bf16[64,1024]{1,0:T(8,128)(2,1)S(1)} %get-tuple-element.14), channel_id=1, source_target_pairs={{0,8},{2,10},{4,12},{6,14},{8,16},{10,18},{12,20},{14,22},{16,24},... | collective-permute-start | bytes 393224 | tf_op jit(solution)/shard_map/ppermute | solution.py:240
  22.5 21.4 %collective-permute-start.2 = (bf16[64,1024]{1,0:T(8,128)(2,1)S(1)}, bf16[64,1024]{1,0:T(8,128)(2,1)S(1)}, u32[]{:S(2)}, u32[]{:S(2)}) collective-permute-start(bf16[64,1024]{1,0:T(8,128)(2,1)S(1)} %get-tuple-element.16), channel_id=1, source_target_pairs={{0,16},{2,18},{4,20},{6,22},{8,24},{10,26},{12,28},{14,30},{16,0},... | collective-permute-start | bytes 393224 | tf_op jit(solution)/shard_map/ppermute | solution.py:240
  44.6 5.6 %collective-permute-start.4 = (bf16[4,16,1024]{2,1,0:T(8,128)(2,1)}, bf16[4,16,1024]{2,1,0:T(8,128)(2,1)S(1)}, u32[]{:S(2)}, u32[]{:S(2)}) collective-permute-start(bf16[4,16,1024]{2,1,0:T(8,128)(2,1)} %get-tuple-element.10), channel_id=1, source_target_pairs={{0,2},{2,4},{4,6},{6,0},{8,10},{10,12},{12,14},{14,8},{16,18},{18,... | collective-permute-start | bytes 393224 | tf_op jit(solution)/shard_map/ppermute | solution.py:255
  44.6 6.4 %collective-permute-start.5 = (bf16[4,16,1024]{2,1,0:T(8,128)(2,1)S(1)}, bf16[4,16,1024]{2,1,0:T(8,128)(2,1)S(1)}, u32[]{:S(2)}, u32[]{:S(2)}) collective-permute-start(bf16[4,16,1024]{2,1,0:T(8,128)(2,1)S(1)} %get-tuple-element.11), channel_id=1, source_target_pairs={{0,4},{2,6},{4,0},{6,2},{8,12},{10,14},{12,8},{14,10},{16,20},{18,... | collective-permute-start | bytes 393224 | tf_op jit(solution)/shard_map/ppermute | solution.py:255
  46.1 6.3 %collective-permute-start.6 = (bf16[4,16,1024]{2,1,0:T(8,128)(2,1)S(1)}, bf16[4,16,1024]{2,1,0:T(8,128)(2,1)S(1)}, u32[]{:S(2)}, u32[]{:S(2)}) collective-permute-start(bf16[4,16,1024]{2,1,0:T(8,128)(2,1)S(1)} %get-tuple-element.12), channel_id=1, source_target_pairs={{0,6},{2,0},{4,2},{6,4},{8,14},{10,8},{12,10},{14,12},{16,22},{18,... | collective-permute-start | bytes 393224 | tf_op jit(solution)/shard_map/ppermute | solution.py:255
  63.6 18.6 %all-to-all-start.1 = ((bf16[16,16,1024]{2,1,0:T(8,128)(2,1)}), bf16[16,16,1024]{2,1,0:T(8,128)(2,1)}, u32[]{:S(2)}, u32[]{:S(2)}) async-start(bf16[16,16,1024]{2,1,0:T(8,128)(2,1)} %convolve.1), calls=%async_computation.1 | async-start | bytes 1048576 | tf_op jit(solution)/shard_map/all_to_all | solution.py:290
  84.5 14.2 %collective-permute-start.7 = (bf16[256,1024]{1,0:T(8,128)(2,1)}, bf16[256,1024]{1,0:T(8,128)(2,1)S(1)}, u32[]{:S(2)}, u32[]{:S(2)}) collective-permute-start(bf16[256,1024]{1,0:T(8,128)(2,1)} %fusion.1), channel_id=1, source_target_pairs={{0,1},{1,0},{2,3},{3,2},{4,5},{5,4},{6,7},{7,6},{8,9},{9,8},{10,11... | collective-permute-start | bytes 1572872 | tf_op jit(solution)/shard_map/ppermute | solution.py:296
where the time goes:
time: 105 us; the launch traced here: 104 us
  waiting for transfers between devices  50.7 us (48%)
  starting transfers between devices  25.2 us (24%)
  Pallas kernels  18.1 us (17%)
  matrix products  5.68 us (5%)
  other arithmetic  2.34 us (2%)
  local copies, waits for them, and re-layouts  2.05 us (2%)
    ppermute x3, waiting for transfers between devices, moved_filter(): lax.ppermute(piece, 'ctx', outer_pairs(step))  20.3 us
    ppermute x1, waiting for transfers between devices, block(): lax.ppermute(gated, 'ch', [(i, (i + step) % halves) for i in range(halves)])  12.7 us
    all_to_all x1, waiting for transfers between devices, block(): lax.all_to_all(result, 'ctx', 0, 0).reshape(channels, tokens).astype(f32)  12.3 us
    pallas_call x1, Pallas kernels, block(): pl.pallas_call(functools.partial(conv_kernel, count=count, channels=own,...  11.2 us
    all_to_all x1, starting transfers between devices, block(): lax.all_to_all(product_kv.reshape(sources, own, tokens), 'ctx', 0, 0)  9.14 us
    dot_general x2, matrix products, block(): part = jnp.einsum('cb,cd->bd', piece, weights, preferred_element_type=f32)  5.68 us
    pallas_call x2, Pallas kernels, featurize(): pl.pallas_call(functools.partial(kernel, width=tap_rows.shape[1] - 1), gr...  5.03 us
    ppermute x3, starting transfers between devices, moved_filter(): lax.ppermute(piece, 'ctx', outer_pairs(step))  4.8 us
  transfers between devices with their start and end apart: 10, of which 9 were waited for; matrix products, arithmetic and copies ran while one was open for 1% of the time, Pallas kernels for 2%

commit v1 on v0

--- a/solution.py
+++ b/solution.py
@@ -12,6 +12,7 @@
 LANES = 128
 GROUP = 8
 STEPS = 2
+CHUNKS = 4
 f32, bf16 = jnp.float32, jnp.bfloat16
 
 
@@ -193,15 +194,54 @@
         out_specs=rows,
         out_shape=jax.ShapeDtypeStruct((channels, tokens), dtype),
         compiler_params=room(12),
-    )(*in_hbm(*arrays), tap_rows, rim)
+    )(*in_hbm(*arrays, tap_rows), rim)
 
 
 def pack_kernel(inner_index, *refs, count, inner, own):
-    pieces, outs = refs[:count], refs[count:]
+    pieces, outs, sems = refs[:count], refs[count:-1], refs[-1]
+    copies = []
     for step in range(inner):
         begin = pl.multiple_of(((inner_index[0] + step) % inner) * own, own)
-        for i in range(count):
-            outs[step][i] = pieces[i][pl.ds(begin, own), :]
+        sources = [piece.at[pl.ds(begin, own)] for piece in pieces]
+        copies += start_copies(sources, [outs[step].at[i] for i in range(count)], sems, step * count)
+    for copy in copies:
+        copy.wait()
+
+
+def gate_kernel(y, q_short, product_kv, skip, *refs):
+    outs, q_held, kv_held, sems = refs[:-3], refs[-3], refs[-2], refs[-1]
+    size = outs[0].shape[1]
+    spans = [pl.ds(i * size, size) for i in range(len(outs))]
+    waits = []
+    for i, span in enumerate(spans):
+        sources = [q_short.at[:, span], product_kv.at[:, span]]
+        waits.append(start_copies(sources, [q_held.at[:, span], kv_held.at[:, span]], sems, 2 * i))
+    gain = columns_of(skip[...])[:, :1]
+    for span, out, copies in zip(spans, outs, waits):
+        for copy in copies:
+            copy.wait()
+        mixed = y[:, span].astype(f32) + gain * kv_held[:, span].astype(f32)
+        out[...] = (q_held[:, span] * mixed).astype(out.dtype)
+
+
+def project_kernel(owners, *refs, count, chunk, aliased):
+    pieces, weights = refs[:count], refs[count]
+    out, held, sems = refs[count + 1 + aliased :]
+    channels, size = pieces[0].shape
+    rows = pl.ds(chunk * size, size)
+    width = min(512, held.shape[1])
+    copies = []
+    for i in range(held.shape[1] // width):
+        span = pl.ds(i * width, width)
+        total = None
+        for piece, k in zip(pieces, range(count)):
+            block = weights[pl.ds(pl.multiple_of(owners[k] * channels, channels), channels), span]
+            part = lax.dot_general(piece[...], block, (((0,), (0,)), ((), ())), preferred_element_type=f32)
+            total = part if total is None else total + part
+        held[:, span] = total.astype(held.dtype)
+        copies += start_copies([held.at[:, span]], [out.at[rows, span]], sems, i)
+    for copy in copies:
+        copy.wait()
 
 
 def in_hbm(*values):
@@ -241,9 +281,10 @@
     if own % 16 == 0:
         packed = pl.pallas_call(
             functools.partial(pack_kernel, count=outer, inner=inner, own=own),
-            in_specs=[smem()] + [vmem()] * outer,
-            out_specs=[vmem()] * inner,
+            in_specs=[smem()] + [pl.BlockSpec(memory_space=pl.ANY)] * outer,
+            out_specs=[pl.BlockSpec(memory_space=pltpu.HBM)] * inner,
             out_shape=[jax.ShapeDtypeStruct((outer, own, tokens), bf16)] * inner,
+            scratch_shapes=[pltpu.SemaphoreType.DMA((outer * inner,))],
             compiler_params=room(8),
             name="pack",
         )(me_inner[None].astype(jnp.int32), *pieces)
@@ -287,18 +328,45 @@
         compiler_params=room(40),
         name="convolve",
     )(order, *arrived, signal_moved, *in_hbm(*used))
-    long_out = lax.all_to_all(result, "ctx", 0, 0).reshape(channels, tokens).astype(f32)
-    gated = (q_short * (long_out + skip_gain[:, None] * product_kv.astype(f32))).astype(bf16)
-
-    mine = lax.axis_index("ch")
-    summed = None
-    for step in range(halves):
-        piece = gated if step == 0 else lax.ppermute(gated, "ch", [(i, (i + step) % halves) for i in range(halves)])
-        owner = (mine - step) % halves
-        weights = lax.dynamic_slice_in_dim(out_weight, owner * channels, channels, axis=0)
-        part = jnp.einsum("cb,cd->bd", piece, weights, preferred_element_type=f32)
-        summed = part if summed is None else summed + part
-    return summed.astype(bf16)
+    long_out = lax.all_to_all(result, "ctx", 0, 0).reshape(channels, tokens)
+    anywhere = pl.BlockSpec(memory_space=pl.ANY)
+    chunks = CHUNKS if tokens % (CHUNKS * LANES) == 0 else 1
+    size = tokens // chunks
+    gated = pl.pallas_call(
+        gate_kernel,
+        in_specs=[vmem(), anywhere, anywhere, vmem()],
+        out_specs=[vmem()] * chunks,
+        out_shape=[jax.ShapeDtypeStruct((channels, size), bf16)] * chunks,
+        scratch_shapes=[
+            pltpu.VMEM((channels, tokens), f32),
+            pltpu.VMEM((channels, tokens), bf16),
+            pltpu.SemaphoreType.DMA((2 * chunks,)),
+        ],
+        compiler_params=room(12),
+        name="gate",
+    )(long_out, *in_hbm(q_short, product_kv), skip_gain[None, :])
+
+    owners = ((lax.axis_index("ch") - jnp.arange(halves)) % halves).astype(jnp.int32)
+    features = out_weight.shape[1]
+    pieces = [[piece] for piece in gated]
+    for step in range(1, halves):
+        for chunk in range(chunks):
+            pairs = [(i, (i + step) % halves) for i in range(halves)]
+            pieces[chunk].append(lax.ppermute(gated[chunk], "ch", pairs))
+    out = ()
+    for chunk in range(chunks):
+        out = pl.pallas_call(
+            functools.partial(project_kernel, count=halves, chunk=chunk, aliased=len(out)),
+            in_specs=[smem()] + [vmem()] * (halves + 1) + [anywhere] * len(out),
+            out_specs=pl.BlockSpec(memory_space=pltpu.HBM),
+            out_shape=jax.ShapeDtypeStruct((tokens, features), bf16),
+            scratch_shapes=[pltpu.VMEM((size, features), bf16), pltpu.SemaphoreType.DMA((max(1, features // 512),))],
+            input_output_aliases={halves + 2: 0} if out else {},
+            compiler_params=room(16),
+            name="project",
+        )(owners, *pieces[chunk], out_weight, *out)
+        out = (out,)
+    return out[0]
 
 
 def solution(mesh):

time: 105 us -> 100 us (0.952)
  waiting for transfers between devices: 50.7 us -> 39.1 us
  Pallas kernels: 18.1 us -> 27.9 us
  starting transfers between devices: 25.2 us -> 30.9 us
  matrix products: 5.68 us -> 0 us
  other arithmetic: 2.34 us -> 0.09 us
    pallas_call x0 -> x5, Pallas kernels: none -> 9.59 us  [the longest x4 8.09 us: block(): pl.pallas_call(functools.partial(project_kernel, count=halves, chunk=chun...]
    ppermute x1 -> x4, waiting for transfers between devices: 12.7 us -> 3.86 us  [block(): pieces[chunk].append(lax.ppermute(gated[chunk], 'ch', pairs))]
    dot_general x2 -> x0, matrix products: 5.68 us -> none  [block(): part = jnp.einsum('cb,cd->bd', piece, weights, preferred_element_type=f32)]
    ppermute x1 -> x4, starting transfers between devices: 1.52 us -> 4.12 us  [block(): pieces[chunk].append(lax.ppermute(gated[chunk], 'ch', pairs))]
    convert_element_type x1 -> x0, other arithmetic: 2.26 us -> none  [block(): (q_short * (long_out + skip_gain[:, None] * product_kv.astype(f32))).asty...]
    all_to_all x1, starting transfers between devices: 4.44 us -> 6.44 us  [block(): long_out = lax.all_to_all(result, 'ctx', 0, 0).reshape(channels, tokens)]
    ppermute x3, waiting for transfers between devices: 20.3 us -> 18.3 us  [moved_filter(): lax.ppermute(piece, 'ctx', outer_pairs(step))]
    convert_element_type x1, local copies, waits for them, and re-layouts: 1.27 us -> 0.07 us  [moved_filter(): lax.dynamic_slice_in_dim(long_filter, (me_outer + step) % outer * group,...]
  transfers between devices with their start and end apart: 10 -> 13, of which waited for: 9 -> 10; matrix products, arithmetic and copies ran while one was open for 1% -> 0% of each run, Pallas kernels for 2% -> 9%
where the time goes in v1:
time: 100 us; the launch traced here: 99.6 us
  waiting for transfers between devices  39.1 us (39%)
  starting transfers between devices  30.9 us (31%)
  Pallas kernels  27.9 us (28%)
  local copies, waits for them, and re-layouts  1.13 us (1%)
    ppermute x3, waiting for transfers between devices, moved_filter(): lax.ppermute(piece, 'ctx', outer_pairs(step))  18.3 us
    all_to_all x1, waiting for transfers between devices, block(): long_out = lax.all_to_all(result, 'ctx', 0, 0).reshape(channels, tokens)  11.4 us
    pallas_call x1, Pallas kernels, block(): pl.pallas_call(functools.partial(conv_kernel, count=count, channels=own,...  11.2 us
    all_to_all x1, starting transfers between devices, block(): lax.all_to_all(product_kv.reshape(sources, own, tokens), 'ctx', 0, 0)  9.27 us
    pallas_call x4, Pallas kernels, block(): pl.pallas_call(functools.partial(project_kernel, count=halves, chunk=chun...  8.09 us
    all_to_all x1, starting transfers between devices, block(): long_out = lax.all_to_all(result, 'ctx', 0, 0).reshape(channels, tokens)  6.44 us
    ppermute x3, starting transfers between devices, moved_filter(): lax.ppermute(piece, 'ctx', outer_pairs(step))  5.7 us
    pallas_call x2, Pallas kernels, featurize(): pl.pallas_call(functools.partial(kernel, width=tap_rows.shape[1] - 1), gr...  5.04 us
  transfers between devices with their start and end apart: 13, of which 10 were waited for; matrix products, arithmetic and copies ran while one was open for 0% of the time, Pallas kernels for 9%

profile of v1, /device:TPU:0, one launch (start us, length us, event | category | flops | bytes accessed | tf_op | source)
XLA Modules:
  0.0 99.6 jit_solution(5228203284900821735)
XLA Ops:
  0.0 0.0 copy-start.3
  0.0 1.1 %edges.1 = bf16[16,256]{1,0:T(8,128)(2,1)S(1)} custom-call(bf16[256,1024]{1,0:T(8,128)(2,1)} %q.3, bf16[256,1024]{1,0:T(8,128)(2,1)} %k.3, bf16[256,1024]{1,0:T(8,128)(2,1)} %v.3), custom_call_target="tpu_custom_call" | custom-call | tf_op jit(solution)/shard_map/edges/pallas_call | solution.py:138
  1.1 2.4 %collective-permute-start.6 = (bf16[16,256]{1,0:T(8,128)(2,1)S(1)}, bf16[16,256]{1,0:T(8,128)(2,1)S(1)}, u32[]{:S(2)}, u32[]{:S(2)}) collective-permute-start(bf16[16,256]{1,0:T(8,128)(2,1)S(1)} %edges.1), channel_id=1, source_target_pairs={{0,2},{2,4},{4,6},{6,8},{8,10},{10,12},{12,14},{14,16},{16,18},{18... | collective-permute-start | bytes 24584 | tf_op jit(solution)/shard_map/ppermute | solution.py:311
  3.5 0.8 collective-permute-done.6.rim
  4.3 3.2 %shard_map.118.product_kv = bf16[256,1024]{1,0:T(8,128)(2,1)} custom-call(bf16[256,1024]{1,0:T(8,128)(2,1)} %k.3, bf16[256,1024]{1,0:T(8,128)(2,1)} %v.3, bf16[3,3,256]{2,1,0:T(4,128)(2,1)} %bitcast.7, bf16[16,256]{1,0:T(8,128)(2,1)S(1)} %collective-permute-done.6.rim), custom_call_target="tpu_custom_call" | custom-call | tf_op jit(solution)/shard_map/pallas_call | solution.py:186
  7.5 0.0 copy-start.2
  7.5 9.3 %all-to-all-start = ((bf16[16,16,1024]{2,1,0:T(8,128)(2,1)}), bf16[16,16,1024]{2,1,0:T(8,128)(2,1)S(1)}, u32[]{:S(2)}, u32[]{:S(2)}) async-start(bf16[16,16,1024]{2,1,0:T(8,128)(2,1)} %bitcast.2), calls=%async_computation | async-start | bytes 1048576 | tf_op jit(solution)/shard_map/all_to_all | solution.py:314
  16.9 0.0 copy-done.3
  16.9 0.1 dynamic-slice_convert_fusion
  17.0 0.0 copy-start
  17.0 1.9 %collective-permute-start = (bf16[64,1024]{1,0:T(8,128)(2,1)S(1)}, bf16[64,1024]{1,0:T(8,128)(2,1)S(1)}, u32[]{:S(2)}, u32[]{:S(2)}) collective-permute-start(bf16[64,1024]{1,0:T(8,128)(2,1)S(1)} %get-tuple-element.22), channel_id=1, source_target_pairs={{0,8},{2,10},{4,12},{6,14},{8,16},{10,18},{12,20},{14,22},{16,24},... | collective-permute-start | bytes 393224 | tf_op jit(solution)/shard_map/ppermute | solution.py:280
  18.9 2.4 %collective-permute-start.1 = (bf16[64,1024]{1,0:T(8,128)(2,1)S(1)}, bf16[64,1024]{1,0:T(8,128)(2,1)S(1)}, u32[]{:S(2)}, u32[]{:S(2)}) collective-permute-start(bf16[64,1024]{1,0:T(8,128)(2,1)S(1)} %get-tuple-element.24), channel_id=1, source_target_pairs={{0,16},{2,18},{4,20},{6,22},{8,24},{10,26},{12,28},{14,30},{16,0},... | collective-permute-start | bytes 393224 | tf_op jit(solution)/shard_map/ppermute | solution.py:280
  21.3 1.5 %collective-permute-start.2 = (bf16[64,1024]{1,0:T(8,128)(2,1)S(1)}, bf16[64,1024]{1,0:T(8,128)(2,1)S(1)}, u32[]{:S(2)}, u32[]{:S(2)}) collective-permute-start(bf16[64,1024]{1,0:T(8,128)(2,1)S(1)} %get-tuple-element.21), channel_id=1, source_target_pairs={{0,24},{2,26},{4,28},{6,30},{8,0},{10,2},{12,4},{14,6},{16,8},{18,... | collective-permute-start | bytes 393224 | tf_op jit(solution)/shard_map/ppermute | solution.py:280
  22.7 10.8 %collective-permute-done.refs_1_ = bf16[64,1024]{1,0:T(8,128)(2,1)S(1)} collective-permute-done((bf16[64,1024]{1,0:T(8,128)(2,1)S(1)}, bf16[64,1024]{1,0:T(8,128)(2,1)S(1)}, u32[]{:S(2)}, u32[]{:S(2)}) %collective-permute-start) | collective-permute-done | bytes 131104 | tf_op jit(solution)/shard_map/ppermute | solution.py:280
  33.6 7.5 %collective-permute-done.1.refs_2_ = bf16[64,1024]{1,0:T(8,128)(2,1)S(1)} collective-permute-done((bf16[64,1024]{1,0:T(8,128)(2,1)S(1)}, bf16[64,1024]{1,0:T(8,128)(2,1)S(1)}, u32[]{:S(2)}, u32[]{:S(2)}) %collective-permute-start.1) | collective-permute-done | bytes 131104 | tf_op jit(solution)/shard_map/ppermute | solution.py:280
  41.0 0.0 collective-permute-done.2.refs_3_
  41.0 1.0 pack.1
  42.0 0.1 collective-permute-start.3
  42.1 1.5 %collective-permute-start.4 = (bf16[4,16,1024]{2,1,0:T(8,128)(2,1)S(1)}, bf16[4,16,1024]{2,1,0:T(8,128)(2,1)S(1)}, u32[]{:S(2)}, u32[]{:S(2)}) collective-permute-start(bf16[4,16,1024]{2,1,0:T(8,128)(2,1)S(1)} %get-tuple-element.15), channel_id=1, source_target_pairs={{0,4},{2,6},{4,0},{6,2},{8,12},{10,14},{12,8},{14,10},{16,20},{18,... | collective-permute-start | bytes 393224 | tf_op jit(solution)/shard_map/ppermute | solution.py:296
  43.6 1.4 %collective-permute-start.5 = (bf16[4,16,1024]{2,1,0:T(8,128)(2,1)S(1)}, bf16[4,16,1024]{2,1,0:T(8,128)(2,1)S(1)}, u32[]{:S(2)}, u32[]{:S(2)}) collective-permute-start(bf16[4,16,1024]{2,1,0:T(8,128)(2,1)S(1)} %get-tuple-element.16), channel_id=1, source_target_pairs={{0,6},{2,0},{4,2},{6,4},{8,14},{10,8},{12,10},{14,12},{16,22},{18,... | collective-permute-start | bytes 393224 | tf_op jit(solution)/shard_map/ppermute | solution.py:296
  45.0 0.1 broadcast_add_fusion
  45.1 0.1 add.89.order
  45.2 2.5 %collective-permute-done.3.refs_1_ = bf16[4,16,1024]{2,1,0:T(8,128)(2,1)S(1)} collective-permute-done((bf16[4,16,1024]{2,1,0:T(8,128)(2,1)}, bf16[4,16,1024]{2,1,0:T(8,128)(2,1)S(1)}, u32[]{:S(2)}, u32[]{:S(2)}) %collective-permute-start.3) | collective-permute-done | bytes 131104 | tf_op jit(solution)/shard_map/ppermute | solution.py:296
  47.6 0.9 collective-permute-done.4.refs_2_
  48.5 1.4 %collective-permute-done.5.refs_3_ = bf16[4,16,1024]{2,1,0:T(8,128)(2,1)S(1)} collective-permute-done((bf16[4,16,1024]{2,1,0:T(8,128)(2,1)S(1)}, bf16[4,16,1024]{2,1,0:T(8,128)(2,1)S(1)}, u32[]{:S(2)}, u32[]{:S(2)}) %collective-permute-start.5) | collective-permute-done | bytes 131104 | tf_op jit(solution)/shard_map/ppermute | solution.py:296
  49.9 0.0 all-to-all-done.refs_4_
  49.9 11.2 %convolve.1 = bf16[16,16,1024]{2,1,0:T(8,128)(2,1)} custom-call(s32[16]{0:T(128)S(1)} %add.89.order, bf16[4,16,1024]{2,1,0:T(8,128)(2,1)S(1)} %get-tuple-element.13.refs_0_, bf16[4,16,1024]{2,1,0:T(8,128)(2,1)S(1)} %collective-permute-done.3.refs_1_, bf16[4,16,1024]{2,1,0:T(8,128)(2,1)S(1)} %collective-permute-done.4.refs_2_, ...), custom_call_target="tpu_custom_call" | custom-call | tf_op jit(solution)/shard_map/convolve/pallas_call | solution.py:320
  61.1 6.4 %all-to-all-start.1 = ((bf16[16,16,1024]{2,1,0:T(8,128)(2,1)}), bf16[16,16,1024]{2,1,0:T(8,128)(2,1)S(1)}, u32[]{:S(2)}, u32[]{:S(2)}) async-start(bf16[16,16,1024]{2,1,0:T(8,128)(2,1)} %convolve.1), calls=%async_computation.1 | async-start | bytes 1048576 | tf_op jit(solution)/shard_map/all_to_all | solution.py:331
  67.6 1.9 %shard_map.119.q_short = f32[256,1024]{1,0:T(8,128)S(1)} custom-call(bf16[256,1024]{1,0:T(8,128)(2,1)} %q.3, bf16[3,3,256]{2,1,0:T(4,128)(2,1)} %bitcast.8, bf16[16,256]{1,0:T(8,128)(2,1)S(1)} %collective-permute-done.6.rim), custom_call_target="tpu_custom_call" | custom-call | tf_op jit(solution)/shard_map/pallas_call | solution.py:186
  69.4 0.0 copy-start.1
  69.4 1.0 copy-done.1
  70.4 11.4 %all-to-all-done.1 = bf16[16,16,1024]{2,1,0:T(8,128)(2,1)S(1)} async-done(((bf16[16,16,1024]{2,1,0:T(8,128)(2,1)}), bf16[16,16,1024]{2,1,0:T(8,128)(2,1)S(1)}, u32[]{:S(2)}, u32[]{:S(2)}) %all-to-all-start.1) | async-done | bytes 524320 | tf_op jit(solution)/shard_map/all_to_all | solution.py:331
  81.8 0.0 copy-done.2
  81.8 1.5 %gate.1 = (bf16[256,256]{1,0:T(8,128)(2,1)S(1)}, bf16[256,256]{1,0:T(8,128)(2,1)S(1)}, bf16[256,256]{1,0:T(8,128)(2,1)S(1)}, bf16[256,256]{1,0:T(8,128)(2,1)S(1)}) custom-call(bf16[256,1024]{1,0:T(8,128)(2,1)S(1)} %bitcast.5, f32[256,1024]{1,0:T(8,128)} %copy-done.1, bf16[256,1024]{1,0:T(8,128)(2,1)} %shard_map.118.product_kv, f32[1,256]{1,0:T(1,128)S(1)} %bitcast.6), custom_call_target="tpu_custom_call" | custom-call | tf_op jit(solution)/shard_map/gate/pallas_call | solution.py:335
  83.3 1.6 %collective-permute-start.10 = (bf16[256,256]{1,0:T(8,128)(2,1)S(1)}, bf16[256,256]{1,0:T(8,128)(2,1)S(1)}, u32[]{:S(2)}, u32[]{:S(2)}) collective-permute-start(bf16[256,256]{1,0:T(8,128)(2,1)S(1)} %get-tuple-element.20.refs_0_), channel_id=1, source_target_pairs={{0,1},{1,0},{2,3},{3,2},{4,5},{5,4},{6,7},{7,6},{8,9},{9,8},{10,11... | collective-permute-start | bytes 393224 | tf_op jit(solution)/shard_map/ppermute | solution.py:355
  84.9 0.5 collective-permute-start.9
  85.4 1.5 %collective-permute-start.8 = (bf16[256,256]{1,0:T(8,128)(2,1)S(1)}, bf16[256,256]{1,0:T(8,128)(2,1)S(1)}, u32[]{:S(2)}, u32[]{:S(2)}) collective-permute-start(bf16[256,256]{1,0:T(8,128)(2,1)S(1)} %get-tuple-element.18.refs_0_), channel_id=1, source_target_pairs={{0,1},{1,0},{2,3},{3,2},{4,5},{5,4},{6,7},{7,6},{8,9},{9,8},{10,11... | collective-permute-start | bytes 393224 | tf_op jit(solution)/shard_map/ppermute | solution.py:355
  86.9 0.5 collective-permute-start.7
  87.5 2.3 %collective-permute-done.10.refs_1_ = bf16[256,256]{1,0:T(8,128)(2,1)S(1)} collective-permute-done((bf16[256,256]{1,0:T(8,128)(2,1)S(1)}, bf16[256,256]{1,0:T(8,128)(2,1)S(1)}, u32[]{:S(2)}, u32[]{:S(2)}) %collective-permute-start.10) | collective-permute-done | bytes 131104 | tf_op jit(solution)/shard_map/ppermute | solution.py:355
  89.8 0.0 copy-done
  89.8 2.0 %project.4.refs_3_ = bf16[1024,2048]{1,0:T(8,128)(2,1)} custom-call(s32[2]{0:T(128)S(1)} %and_select_fusion.2.owners, bf16[256,256]{1,0:T(8,128)(2,1)S(1)} %get-tuple-element.20.refs_0_, bf16[256,256]{1,0:T(8,128)(2,1)S(1)} %collective-permute-done.10.refs_1_, bf16[512,2048]{1,0:T(8,128)(2,1)S(1)} %copy-done), custom_call_target="tpu_custom_call" | custom-call | tf_op jit(solution)/shard_map/project/pallas_call | solution.py:358
  91.8 0.8 collective-permute-done.9.refs_1_
  92.6 2.0 %project.5.refs_3_ = bf16[1024,2048]{1,0:T(8,128)(2,1)} custom-call(s32[2]{0:T(128)S(1)} %and_select_fusion.2.owners, bf16[256,256]{1,0:T(8,128)(2,1)S(1)} %get-tuple-element.19.refs_0_, bf16[256,256]{1,0:T(8,128)(2,1)S(1)} %collective-permute-done.9.refs_1_, bf16[512,2048]{1,0:T(8,128)(2,1)S(1)} %copy-done, ...), custom_call_target="tpu_custom_call", output_to_operand_aliasing={{}: (4, {})} | custom-call | tf_op jit(solution)/shard_map/project/pallas_call | solution.py:358
  94.6 0.8 collective-permute-done.8.refs_1_
  95.4 2.0 %project.6.refs_3_ = bf16[1024,2048]{1,0:T(8,128)(2,1)} custom-call(s32[2]{0:T(128)S(1)} %and_select_fusion.2.owners, bf16[256,256]{1,0:T(8,128)(2,1)S(1)} %get-tuple-element.18.refs_0_, bf16[256,256]{1,0:T(8,128)(2,1)S(1)} %collective-permute-done.8.refs_1_, bf16[512,2048]{1,0:T(8,128)(2,1)S(1)} %copy-done, ...), custom_call_target="tpu_custom_call", output_to_operand_aliasing={{}: (4, {})} | custom-call | tf_op jit(solution)/shard_map/project/pallas_call | solution.py:358
  97.4 0.0 collective-permute-done.7.refs_1_
  97.4 2.0 %project.7 = bf16[1024,2048]{1,0:T(8,128)(2,1)} custom-call(s32[2]{0:T(128)S(1)} %and_select_fusion.2.owners, bf16[256,256]{1,0:T(8,128)(2,1)S(1)} %get-tuple-element.17.refs_0_, bf16[256,256]{1,0:T(8,128)(2,1)S(1)} %collective-permute-done.7.refs_1_, bf16[512,2048]{1,0:T(8,128)(2,1)S(1)} %copy-done, ...), custom_call_target="tpu_custom_call", output_to_operand_aliasing={{}: (4, {})} | custom-call | tf_op jit(solution)/shard_map/project/pallas_call | solution.py:358
  (2 shorter events, 0.0 us)
Async XLA Ops:
  0.0 16.9 %copy-start.3 = (f32[256,1024]{1,0:T(8,128)S(1)}, f32[256,1024]{1,0:T(8,128)}, u32[]{:S(2)}) copy-start(f32[256,1024]{1,0:T(8,128)} %param.16) | copy-start | bytes 3145732
  1.1 3.2 %collective-permute-start.6 = (bf16[16,256]{1,0:T(8,128)(2,1)S(1)}, bf16[16,256]{1,0:T(8,128)(2,1)S(1)}, u32[]{:S(2)}, u32[]{:S(2)}) collective-permute-start(bf16[16,256]{1,0:T(8,128)(2,1)S(1)} %edges.1), channel_id=1, source_target_pairs={{0,2},{2,4},{4,6},{6,8},{8,10},{10,12},{12,14},{14,16},{16,18},{18... | collective-permute-start | bytes 24584 | tf_op jit(solution)/shard_map/ppermute | solution.py:311
  7.5 74.3 %copy-start.2 = (f32[256]{0:T(256)S(1)}, f32[256]{0:T(256)}, u32[]{:S(2)}) copy-start(f32[256]{0:T(256)} %param.17) | copy-start | bytes 3076
  7.5 42.3 %all-to-all-start = ((bf16[16,16,1024]{2,1,0:T(8,128)(2,1)}), bf16[16,16,1024]{2,1,0:T(8,128)(2,1)S(1)}, u32[]{:S(2)}, u32[]{:S(2)}) async-start(bf16[16,16,1024]{2,1,0:T(8,128)(2,1)} %bitcast.2), calls=%async_computation | async-start | bytes 1048576 | tf_op jit(solution)/shard_map/all_to_all | solution.py:314
  17.0 72.8 %copy-start = (bf16[512,2048]{1,0:T(8,128)(2,1)S(1)}, bf16[512,2048]{1,0:T(8,128)(2,1)}, u32[]{:S(2)}) copy-start(bf16[512,2048]{1,0:T(8,128)(2,1)} %refs_2_.7) | copy-start | bytes 6291460
  17.0 16.6 %collective-permute-start = (bf16[64,1024]{1,0:T(8,128)(2,1)S(1)}, bf16[64,1024]{1,0:T(8,128)(2,1)S(1)}, u32[]{:S(2)}, u32[]{:S(2)}) collective-permute-start(bf16[64,1024]{1,0:T(8,128)(2,1)S(1)} %get-tuple-element.22), channel_id=1, source_target_pairs={{0,8},{2,10},{4,12},{6,14},{8,16},{10,18},{12,20},{14,22},{16,24},... | collective-permute-start | bytes 393224 | tf_op jit(solution)/shard_map/ppermute | solution.py:280
  18.9 22.2 %collective-permute-start.1 = (bf16[64,1024]{1,0:T(8,128)(2,1)S(1)}, bf16[64,1024]{1,0:T(8,128)(2,1)S(1)}, u32[]{:S(2)}, u32[]{:S(2)}) collective-permute-start(bf16[64,1024]{1,0:T(8,128)(2,1)S(1)} %get-tuple-element.24), channel_id=1, source_target_pairs={{0,16},{2,18},{4,20},{6,22},{8,24},{10,26},{12,28},{14,30},{16,0},... | collective-permute-start | bytes 393224 | tf_op jit(solution)/shard_map/ppermute | solution.py:280
  21.3 19.8 %collective-permute-start.2 = (bf16[64,1024]{1,0:T(8,128)(2,1)S(1)}, bf16[64,1024]{1,0:T(8,128)(2,1)S(1)}, u32[]{:S(2)}, u32[]{:S(2)}) collective-permute-start(bf16[64,1024]{1,0:T(8,128)(2,1)S(1)} %get-tuple-element.21), channel_id=1, source_target_pairs={{0,24},{2,26},{4,28},{6,30},{8,0},{10,2},{12,4},{14,6},{16,8},{18,... | collective-permute-start | bytes 393224 | tf_op jit(solution)/shard_map/ppermute | solution.py:280
  42.0 5.6 %collective-permute-start.3 = (bf16[4,16,1024]{2,1,0:T(8,128)(2,1)}, bf16[4,16,1024]{2,1,0:T(8,128)(2,1)S(1)}, u32[]{:S(2)}, u32[]{:S(2)}) collective-permute-start(bf16[4,16,1024]{2,1,0:T(8,128)(2,1)} %get-tuple-element.14), channel_id=1, source_target_pairs={{0,2},{2,4},{4,6},{6,0},{8,10},{10,12},{12,14},{14,8},{16,18},{18,... | collective-permute-start | bytes 393224 | tf_op jit(solution)/shard_map/ppermute | solution.py:296
  42.1 6.4 %collective-permute-start.4 = (bf16[4,16,1024]{2,1,0:T(8,128)(2,1)S(1)}, bf16[4,16,1024]{2,1,0:T(8,128)(2,1)S(1)}, u32[]{:S(2)}, u32[]{:S(2)}) collective-permute-start(bf16[4,16,1024]{2,1,0:T(8,128)(2,1)S(1)} %get-tuple-element.15), channel_id=1, source_target_pairs={{0,4},{2,6},{4,0},{6,2},{8,12},{10,14},{12,8},{14,10},{16,20},{18,... | collective-permute-start | bytes 393224 | tf_op jit(solution)/shard_map/ppermute | solution.py:296
  43.6 6.3 %collective-permute-start.5 = (bf16[4,16,1024]{2,1,0:T(8,128)(2,1)S(1)}, bf16[4,16,1024]{2,1,0:T(8,128)(2,1)S(1)}, u32[]{:S(2)}, u32[]{:S(2)}) collective-permute-start(bf16[4,16,1024]{2,1,0:T(8,128)(2,1)S(1)} %get-tuple-element.16), channel_id=1, source_target_pairs={{0,6},{2,0},{4,2},{6,4},{8,14},{10,8},{12,10},{14,12},{16,22},{18,... | collective-permute-start | bytes 393224 | tf_op jit(solution)/shard_map/ppermute | solution.py:296
  61.1 20.7 %all-to-all-start.1 = ((bf16[16,16,1024]{2,1,0:T(8,128)(2,1)}), bf16[16,16,1024]{2,1,0:T(8,128)(2,1)S(1)}, u32[]{:S(2)}, u32[]{:S(2)}) async-start(bf16[16,16,1024]{2,1,0:T(8,128)(2,1)} %convolve.1), calls=%async_computation.1 | async-start | bytes 1048576 | tf_op jit(solution)/shard_map/all_to_all | solution.py:331
  69.4 1.0 copy-start.1
  83.3 6.4 %collective-permute-start.10 = (bf16[256,256]{1,0:T(8,128)(2,1)S(1)}, bf16[256,256]{1,0:T(8,128)(2,1)S(1)}, u32[]{:S(2)}, u32[]{:S(2)}) collective-permute-start(bf16[256,256]{1,0:T(8,128)(2,1)S(1)} %get-tuple-element.20.refs_0_), channel_id=1, source_target_pairs={{0,1},{1,0},{2,3},{3,2},{4,5},{5,4},{6,7},{7,6},{8,9},{9,8},{10,11... | collective-permute-start | bytes 393224 | tf_op jit(solution)/shard_map/ppermute | solution.py:355
  84.9 7.7 %collective-permute-start.9 = (bf16[256,256]{1,0:T(8,128)(2,1)S(1)}, bf16[256,256]{1,0:T(8,128)(2,1)S(1)}, u32[]{:S(2)}, u32[]{:S(2)}) collective-permute-start(bf16[256,256]{1,0:T(8,128)(2,1)S(1)} %get-tuple-element.19.refs_0_), channel_id=1, source_target_pairs={{0,1},{1,0},{2,3},{3,2},{4,5},{5,4},{6,7},{7,6},{8,9},{9,8},{10,11... | collective-permute-start | bytes 393224 | tf_op jit(solution)/shard_map/ppermute | solution.py:355
  85.4 10.0 %collective-permute-start.8 = (bf16[256,256]{1,0:T(8,128)(2,1)S(1)}, bf16[256,256]{1,0:T(8,128)(2,1)S(1)}, u32[]{:S(2)}, u32[]{:S(2)}) collective-permute-start(bf16[256,256]{1,0:T(8,128)(2,1)S(1)} %get-tuple-element.18.refs_0_), channel_id=1, source_target_pairs={{0,1},{1,0},{2,3},{3,2},{4,5},{5,4},{6,7},{7,6},{8,9},{9,8},{10,11... | collective-permute-start | bytes 393224 | tf_op jit(solution)/shard_map/ppermute | solution.py:355
  86.9 10.5 %collective-permute-start.7 = (bf16[256,256]{1,0:T(8,128)(2,1)S(1)}, bf16[256,256]{1,0:T(8,128)(2,1)S(1)}, u32[]{:S(2)}, u32[]{:S(2)}) collective-permute-start(bf16[256,256]{1,0:T(8,128)(2,1)S(1)} %get-tuple-element.17.refs_0_), channel_id=1, source_target_pairs={{0,1},{1,0},{2,3},{3,2},{4,5},{5,4},{6,7},{7,6},{8,9},{9,8},{10,11... | collective-permute-start | bytes 393224 | tf_op jit(solution)/shard_map/ppermute | solution.py:355
